TPU v7x, 32 devices: a whole 2x2x4 slice. The times are simulated.
32 devices in a mesh: beam: 8 (over y, x, core), mp: 4 (over z).
Axes of the slice: x: 2, y: 2, z: 4, core: 2. Of those that a mesh axis runs over, the one named last changes fastest.
Arguments:
- queries: bfloat16 [128, 128, 8192], P('beam', None, 'mp'), may hold values from -10 to 10
- new_kv: bfloat16 [128, 2, 128, 1024], P('beam', None, None, 'mp'), may hold values from -6 to 6
- newest_key_value: bfloat16 [128, 2, 128, 1024], P('beam', None, None, 'mp'), may hold values from -6 to 6
- ancestor_block_store: bfloat16 [96, 2, 128, 1024], P('beam', None, None, 'mp'), may hold values from -6 to 6
- parent: int32 [128], replicated, may hold values from 0 to 127, as said below
- ancestors: int32 [128, 5], P('beam'), may hold values from 0 to 95, as said below
- ancestor_count: int32 [128], P('beam'), may hold values from 1 to 5, as said below
- keep_list: int32 [64], replicated, may hold values from 0 to 127, as said below
- w_reward: bfloat16 [8192], P('mp'), may hold values from -0.0625 to 0.0625
Outputs:
- reward: float32 [128, 128], P('beam')
- kept_blocks: bfloat16 [64, 2, 128, 1024], P('beam', None, None, 'mp')
Inputs may be any that keep to these rules, and one draw needn't show every extreme that they name: Each parent has exactly 2 children, consecutive beams of one device starting at a multiple of 2. The groups of children on one device have parents on distinct devices if there are at most as many groups on a device as devices; otherwise at most 2 groups share a parent device, and on every device some 2 do. `keep_list`: distinct beams; survivor j goes to device j // 8. The survivors bound for one device come from distinct devices if there are at most as many of them as devices; otherwise at most 2 come from one device, and on every device some 2 do. `ancestors`: 5 distinct blocks per beam, all among the 12 pool blocks held by the beam's own device. `ancestor_count`: every device has a beam with all 5 slots live.
All inputs are finite; a program needn't handle non-finite values.
Results may differ from a plain program's by a relative error of at most 0.0049.
Values may be sent and summed in bfloat16 or wider, within the bound.
No kernel may reach another device: no remote copies, remote signals or barrier semaphores. Data moves between devices by JAX's collectives and lax.ppermute only.
A program may use at most 128 MiB of HBM per device.

v0:
```python
import jax
import jax.numpy as jnp
from jax import lax
from jax.sharding import PartitionSpec as P

HEAD_SIZE = 128
CHILD = 2


def slot_plan(holder, own_index, capacity):
    is_mine = (holder == own_index).astype(jnp.int32)
    before = jnp.cumsum(is_mine, axis=1) - is_mine
    slot_ids = jnp.arange(capacity, dtype=jnp.int32)
    matches = is_mine[:, None, :] * (before[:, None, :] == slot_ids[None, :, None]).astype(
        jnp.int32
    )
    item_ids = jnp.arange(holder.shape[1], dtype=jnp.int32)
    picked = jnp.sum(matches * item_ids[None, None, :], axis=2)
    filled = jnp.sum(matches, axis=2)
    return (picked, filled)


def slot_lookup(row_holder, capacity):
    item_ids = jnp.arange(row_holder.shape[0], dtype=jnp.int32)
    earlier = (row_holder[:, None] == row_holder[None, :]) & (item_ids[None, :] < item_ids[:, None])
    return row_holder * capacity + jnp.sum(earlier.astype(jnp.int32), axis=1)


def pack_rows(source, local_rows, picked, filled):
    chosen = jnp.take_along_axis(local_rows, picked, axis=1).reshape(-1)
    gathered = jnp.take(source, chosen, axis=0)
    is_live = (filled.reshape(-1) > 0).reshape((-1,) + (1,) * (source.ndim - 1))
    return jnp.where(is_live, gathered, jnp.zeros_like(gathered))


def on_device(
    queries,
    new_kv,
    newest_key_value,
    ancestor_block_store,
    parent,
    ancestors,
    ancestor_count,
    keep_list,
    w_reward,
):
    devices_beam = lax.axis_size("beam")
    own_index = lax.axis_index("beam")
    beam_dev = new_kv.shape[0]
    groups_dev = beam_dev // CHILD
    per_peer = -(-groups_dev // devices_beam)
    parent_grid = parent.reshape(devices_beam, beam_dev)
    leaders = parent_grid.reshape(devices_beam, groups_dev, CHILD)[:, :, 0]
    holder = leaders // beam_dev
    picked, filled = slot_plan(holder, own_index, per_peer)
    outgoing = pack_rows(newest_key_value, leaders % beam_dev, picked, filled)
    arrived = lax.all_to_all(outgoing, "beam", split_axis=0, concat_axis=0, tiled=True)
    own_row = lax.dynamic_index_in_dim(holder, own_index, 0, keepdims=False)
    group_kv = jnp.take(arrived, slot_lookup(own_row, per_peer), axis=0)
    parent_kv = jnp.repeat(group_kv, CHILD, axis=0)
    keep_grid = keep_list.reshape(devices_beam, keep_list.shape[0] // devices_beam)
    keep_holder = keep_grid // beam_dev
    picked_keep, filled_keep = slot_plan(keep_holder, own_index, per_peer)
    leaving = pack_rows(new_kv, keep_grid % beam_dev, picked_keep, filled_keep)
    landed = lax.all_to_all(leaving, "beam", split_axis=0, concat_axis=0, tiled=True)
    keep_row = lax.dynamic_index_in_dim(keep_holder, own_index, 0, keepdims=False)
    kept_blocks = jnp.take(landed, slot_lookup(keep_row, per_peer), axis=0)
    block_len = new_kv.shape[2]
    kv_heads = new_kv.shape[3] // HEAD_SIZE
    q_heads = queries.shape[2] // HEAD_SIZE
    per_group = q_heads // kv_heads
    slots_total = ancestors.shape[1]
    total_key_count = (slots_total + 2) * block_len
    key_slot = jnp.arange(total_key_count) // block_len
    key_pos = jnp.arange(total_key_count) % block_len
    tok_pos = jnp.arange(block_len)
    local_ids = ancestors - own_index * ancestor_block_store.shape[0]
    pair_size = 2
    steps_count = beam_dev // pair_size

    def fold_pairs(tensor):
        return tensor.reshape((steps_count, pair_size) + tensor.shape[1:])

    def attend_pair(pieces):
        current_query_block, own_block, parent_block, block_ids, live_count = pieces
        block_list = jnp.concatenate(
            [
                jnp.take(ancestor_block_store, block_ids, axis=0),
                parent_block[:, None],
                own_block[:, None],
            ],
            axis=1,
        )
        key_row_matrix = block_list[:, :, 0].reshape(
            pair_size, total_key_count, kv_heads, HEAD_SIZE
        )
        value_row_matrix = block_list[:, :, 1].reshape(
            pair_size, total_key_count, kv_heads, HEAD_SIZE
        )
        query_row_matrix = current_query_block.reshape(
            pair_size, block_len, kv_heads, per_group, HEAD_SIZE
        )
        scores = jnp.einsum(
            "btkgd,bjkd->bkgtj",
            query_row_matrix,
            key_row_matrix,
            preferred_element_type=jnp.float32,
        ) * HEAD_SIZE ** (-0.5)
        ancestor_ok = key_slot[None, :] < live_count[:, None]
        causal_ok = key_pos[None, :] <= tok_pos[:, None]
        allowed = jnp.where(
            (key_slot < slots_total)[None, None, :],
            ancestor_ok[:, None, :],
            jnp.where((key_slot == slots_total)[None, None, :], True, causal_ok[None, :, :]),
        )
        scores = jnp.where(allowed[:, None, None], scores, -jnp.inf)
        highest = jnp.max(scores, axis=-1, keepdims=True)
        weights = jnp.exp(scores - highest)
        probabilities = (weights / jnp.sum(weights, axis=-1, keepdims=True)).astype(jnp.bfloat16)
        mixture = jnp.einsum(
            "bkgtj,bjkd->btkgd", probabilities, value_row_matrix, preferred_element_type=jnp.float32
        )
        attended = mixture.astype(jnp.bfloat16).reshape(pair_size * block_len, q_heads * HEAD_SIZE)
        partial_value = jnp.dot(attended, w_reward, preferred_element_type=jnp.float32)
        return partial_value.reshape(pair_size, block_len)

    partial_reward = lax.map(
        attend_pair,
        (
            fold_pairs(queries),
            fold_pairs(new_kv),
            fold_pairs(parent_kv),
            fold_pairs(local_ids),
            fold_pairs(ancestor_count),
        ),
    ).reshape(beam_dev, block_len)
    reward = lax.psum(partial_reward, "mp")
    return (reward, kept_blocks)


def solution(mesh):
    placed = (
        P("beam", None, "mp"),
        P("beam", None, None, "mp"),
        P("beam", None, None, "mp"),
        P("beam", None, None, "mp"),
        P(),
        P("beam", None),
        P("beam"),
        P(),
        P("mp"),
    )
    return jax.shard_map(
        on_device,
        mesh=mesh,
        in_specs=placed,
        out_specs=(P("beam", None), P("beam", None, None, "mp")),
        check_vma=False,
    )
```

profile of v0, /device:TPU:2, one launch (start us, length us, event | category | flops | bytes accessed | tf_op | source)
XLA Modules:
  0.0 298.9 jit_solution(12969944822286315311)
XLA Ops:
  6.4 4.3 %all-to-all-start = ((bf16[8,2,128,256]{3,2,1,0:T(8,128)(2,1)}), bf16[8,2,128,256]{3,2,1,0:T(8,128)(2,1)S(1)}, u32[]{:S(2)}, u32[]{:S(2)}) async-start(bf16[8,2,128,256]{3,2,1,0:T(8,128)(2,1)} %select_select_fusion.1), calls=%async_computation | async-start | bytes 2097152 | tf_op jit(solution)/shard_map/all_to_all | solution.py:57
  11.0 12.3 %copy.32 = bf16[16,128,2048]{1,2,0:T(8,128)(2,1)} copy(bf16[16,128,2048]{2,1,0:T(8,128)(2,1)} %param.17) | data formatting | bytes 16777216 | tf_op args[0]
  23.4 3.2 %gather_fusion.5 = bf16[8,2,128,256]{3,2,1,0:T(8,128)(2,1)} fusion(bf16[16,2,128,256]{3,2,1,0:T(8,128)(2,1)} %param.18, s32[1024]{0:T(1024)S(1)} %pad_clamp_fusion.2), kind=kCustom, calls=%fused_computation.5.clone | custom fusion | bytes 2097184 | tf_op jit(solution)/shard_map/jit(_take)/gather | solution.py:31
  26.8 2.4 select_select_fusion
  30.1 4.2 %all-to-all-start.1 = ((bf16[8,2,128,256]{3,2,1,0:T(8,128)(2,1)}), bf16[8,2,128,256]{3,2,1,0:T(8,128)(2,1)}, u32[]{:S(2)}, u32[]{:S(2)}) async-start(bf16[8,2,128,256]{3,2,1,0:T(8,128)(2,1)} %select_select_fusion), calls=%async_computation.1 | async-start | bytes 2097152 | tf_op jit(solution)/shard_map/all_to_all | solution.py:65
  34.3 1.8 gather_fusion.3
  37.9 245.3 %while.12 = (s32[]{:T(128)}, f32[8,2,128]{2,1,0:T(2,128)S(1)}, s32[8,2,5]{2,1,0:T(2,128)S(1)}, bf16[12,2,128,256]{3,2,1,0:T(8,128)(2,1)}, bf16[8,2,2,128,256]{4,...) while((s32[]{:T(128)}, f32[8,2,128]{2,1,0:T(2,128)S(1)}, ...), condition=%wide.region_7.11_spmd.clone.clone, body=%wide.region_4.10_spmd.clone.clone.sunk | while | flops 1909292800 | bytes 54501824 | solution.py:127
  38.0 2.0 gather_fusion
  42.6 2.9 squeeze.42
  45.5 2.3 constant_dynamic-slice_fusion.4
  49.0 11.2 %fusion.92 = (f32[2,2,8,128]{3,2,1,0:T(8,128)S(1)}, f32[2,2,8,128,896]{3,4,2,1,0:T(8,128)}) fusion(pred[2,128,896]{1,2,0:T(8,128)(4,1)S(1)} %broadcast_select_fusion.4, bf16[2,128,2,8,128]{1,4,3,2,0:T(8,128)(2,1)} %bitcast.124, bf16[2,896,2,128,1]{3,2,1,0,4:T(2,128)(2,1)} %bitcast.126), kind=kOutput, calls=%fused_computation.123.clone.1 | convolution fusion | flops 954205056 | bytes 16891904 | tf_op jit(solution)/shard_map/while/body/eval_jaxpr/sub | solution.py:118
  61.3 7.0 %fusion.93 = bf16[2,2,128,8,128]{4,2,3,1,0:T(8,128)(2,1)S(1)} fusion(f32[2,2,8,128,896]{3,4,2,1,0:T(8,128)} %get-tuple-element.237, f32[2,2,8,128]{3,2,1,0:T(8,128)S(1)} %get-tuple-element.238, bf16[2,896,2,128,1]{3,2,1,0,4:T(2,128)(2,1)} %bitcast.127), kind=kOutput, calls=%fused_computation.21.clone.1 | convolution fusion | flops 947388416 | bytes 16662528 | tf_op jit(solution)/shard_map/while/body/eval_jaxpr/bkgtj,bjkd->btkgd/dot_general | solution.py:120
  68.7 2.0 gather_fusion
  73.3 2.9 squeeze.42
  76.2 2.3 constant_dynamic-slice_fusion.4
  79.7 11.2 %fusion.92 = (f32[2,2,8,128]{3,2,1,0:T(8,128)S(1)}, f32[2,2,8,128,896]{3,4,2,1,0:T(8,128)}) fusion(pred[2,128,896]{1,2,0:T(8,128)(4,1)S(1)} %broadcast_select_fusion.4, bf16[2,128,2,8,128]{1,4,3,2,0:T(8,128)(2,1)} %bitcast.124, bf16[2,896,2,128,1]{3,2,1,0,4:T(2,128)(2,1)} %bitcast.126), kind=kOutput, calls=%fused_computation.123.clone.1 | convolution fusion | flops 954205056 | bytes 16891904 | tf_op jit(solution)/shard_map/while/body/eval_jaxpr/sub | solution.py:118
  92.0 7.0 %fusion.93 = bf16[2,2,128,8,128]{4,2,3,1,0:T(8,128)(2,1)S(1)} fusion(f32[2,2,8,128,896]{3,4,2,1,0:T(8,128)} %get-tuple-element.237, f32[2,2,8,128]{3,2,1,0:T(8,128)S(1)} %get-tuple-element.238, bf16[2,896,2,128,1]{3,2,1,0,4:T(2,128)(2,1)} %bitcast.127), kind=kOutput, calls=%fused_computation.21.clone.1 | convolution fusion | flops 947388416 | bytes 16662528 | tf_op jit(solution)/shard_map/while/body/eval_jaxpr/bkgtj,bjkd->btkgd/dot_general | solution.py:120
  99.4 2.0 gather_fusion
  103.9 2.9 squeeze.42
  106.9 2.3 constant_dynamic-slice_fusion.4
  110.4 11.2 %fusion.92 = (f32[2,2,8,128]{3,2,1,0:T(8,128)S(1)}, f32[2,2,8,128,896]{3,4,2,1,0:T(8,128)}) fusion(pred[2,128,896]{1,2,0:T(8,128)(4,1)S(1)} %broadcast_select_fusion.4, bf16[2,128,2,8,128]{1,4,3,2,0:T(8,128)(2,1)} %bitcast.124, bf16[2,896,2,128,1]{3,2,1,0,4:T(2,128)(2,1)} %bitcast.126), kind=kOutput, calls=%fused_computation.123.clone.1 | convolution fusion | flops 954205056 | bytes 16891904 | tf_op jit(solution)/shard_map/while/body/eval_jaxpr/sub | solution.py:118
  122.7 7.0 %fusion.93 = bf16[2,2,128,8,128]{4,2,3,1,0:T(8,128)(2,1)S(1)} fusion(f32[2,2,8,128,896]{3,4,2,1,0:T(8,128)} %get-tuple-element.237, f32[2,2,8,128]{3,2,1,0:T(8,128)S(1)} %get-tuple-element.238, bf16[2,896,2,128,1]{3,2,1,0,4:T(2,128)(2,1)} %bitcast.127), kind=kOutput, calls=%fused_computation.21.clone.1 | convolution fusion | flops 947388416 | bytes 16662528 | tf_op jit(solution)/shard_map/while/body/eval_jaxpr/bkgtj,bjkd->btkgd/dot_general | solution.py:120
  130.0 2.0 gather_fusion
  134.6 2.9 squeeze.42
  137.5 2.3 constant_dynamic-slice_fusion.4
  141.0 11.2 %fusion.92 = (f32[2,2,8,128]{3,2,1,0:T(8,128)S(1)}, f32[2,2,8,128,896]{3,4,2,1,0:T(8,128)}) fusion(pred[2,128,896]{1,2,0:T(8,128)(4,1)S(1)} %broadcast_select_fusion.4, bf16[2,128,2,8,128]{1,4,3,2,0:T(8,128)(2,1)} %bitcast.124, bf16[2,896,2,128,1]{3,2,1,0,4:T(2,128)(2,1)} %bitcast.126), kind=kOutput, calls=%fused_computation.123.clone.1 | convolution fusion | flops 954205056 | bytes 16891904 | tf_op jit(solution)/shard_map/while/body/eval_jaxpr/sub | solution.py:118
  153.3 7.0 %fusion.93 = bf16[2,2,128,8,128]{4,2,3,1,0:T(8,128)(2,1)S(1)} fusion(f32[2,2,8,128,896]{3,4,2,1,0:T(8,128)} %get-tuple-element.237, f32[2,2,8,128]{3,2,1,0:T(8,128)S(1)} %get-tuple-element.238, bf16[2,896,2,128,1]{3,2,1,0,4:T(2,128)(2,1)} %bitcast.127), kind=kOutput, calls=%fused_computation.21.clone.1 | convolution fusion | flops 947388416 | bytes 16662528 | tf_op jit(solution)/shard_map/while/body/eval_jaxpr/bkgtj,bjkd->btkgd/dot_general | solution.py:120
  160.7 2.0 gather_fusion
  165.3 2.9 squeeze.42
  168.2 2.3 constant_dynamic-slice_fusion.4
  171.7 11.2 %fusion.92 = (f32[2,2,8,128]{3,2,1,0:T(8,128)S(1)}, f32[2,2,8,128,896]{3,4,2,1,0:T(8,128)}) fusion(pred[2,128,896]{1,2,0:T(8,128)(4,1)S(1)} %broadcast_select_fusion.4, bf16[2,128,2,8,128]{1,4,3,2,0:T(8,128)(2,1)} %bitcast.124, bf16[2,896,2,128,1]{3,2,1,0,4:T(2,128)(2,1)} %bitcast.126), kind=kOutput, calls=%fused_computation.123.clone.1 | convolution fusion | flops 954205056 | bytes 16891904 | tf_op jit(solution)/shard_map/while/body/eval_jaxpr/sub | solution.py:118
  184.0 7.0 %fusion.93 = bf16[2,2,128,8,128]{4,2,3,1,0:T(8,128)(2,1)S(1)} fusion(f32[2,2,8,128,896]{3,4,2,1,0:T(8,128)} %get-tuple-element.237, f32[2,2,8,128]{3,2,1,0:T(8,128)S(1)} %get-tuple-element.238, bf16[2,896,2,128,1]{3,2,1,0,4:T(2,128)(2,1)} %bitcast.127), kind=kOutput, calls=%fused_computation.21.clone.1 | convolution fusion | flops 947388416 | bytes 16662528 | tf_op jit(solution)/shard_map/while/body/eval_jaxpr/bkgtj,bjkd->btkgd/dot_general | solution.py:120
  191.3 2.0 gather_fusion
  195.9 2.9 squeeze.42
  198.8 2.3 constant_dynamic-slice_fusion.4
  202.4 11.2 %fusion.92 = (f32[2,2,8,128]{3,2,1,0:T(8,128)S(1)}, f32[2,2,8,128,896]{3,4,2,1,0:T(8,128)}) fusion(pred[2,128,896]{1,2,0:T(8,128)(4,1)S(1)} %broadcast_select_fusion.4, bf16[2,128,2,8,128]{1,4,3,2,0:T(8,128)(2,1)} %bitcast.124, bf16[2,896,2,128,1]{3,2,1,0,4:T(2,128)(2,1)} %bitcast.126), kind=kOutput, calls=%fused_computation.123.clone.1 | convolution fusion | flops 954205056 | bytes 16891904 | tf_op jit(solution)/shard_map/while/body/eval_jaxpr/sub | solution.py:118
  214.6 7.0 %fusion.93 = bf16[2,2,128,8,128]{4,2,3,1,0:T(8,128)(2,1)S(1)} fusion(f32[2,2,8,128,896]{3,4,2,1,0:T(8,128)} %get-tuple-element.237, f32[2,2,8,128]{3,2,1,0:T(8,128)S(1)} %get-tuple-element.238, bf16[2,896,2,128,1]{3,2,1,0,4:T(2,128)(2,1)} %bitcast.127), kind=kOutput, calls=%fused_computation.21.clone.1 | convolution fusion | flops 947388416 | bytes 16662528 | tf_op jit(solution)/shard_map/while/body/eval_jaxpr/bkgtj,bjkd->btkgd/dot_general | solution.py:120
  222.0 2.0 gather_fusion
  226.6 2.9 squeeze.42
  229.5 2.3 constant_dynamic-slice_fusion.4
  233.0 11.2 %fusion.92 = (f32[2,2,8,128]{3,2,1,0:T(8,128)S(1)}, f32[2,2,8,128,896]{3,4,2,1,0:T(8,128)}) fusion(pred[2,128,896]{1,2,0:T(8,128)(4,1)S(1)} %broadcast_select_fusion.4, bf16[2,128,2,8,128]{1,4,3,2,0:T(8,128)(2,1)} %bitcast.124, bf16[2,896,2,128,1]{3,2,1,0,4:T(2,128)(2,1)} %bitcast.126), kind=kOutput, calls=%fused_computation.123.clone.1 | convolution fusion | flops 954205056 | bytes 16891904 | tf_op jit(solution)/shard_map/while/body/eval_jaxpr/sub | solution.py:118
  245.3 7.0 %fusion.93 = bf16[2,2,128,8,128]{4,2,3,1,0:T(8,128)(2,1)S(1)} fusion(f32[2,2,8,128,896]{3,4,2,1,0:T(8,128)} %get-tuple-element.237, f32[2,2,8,128]{3,2,1,0:T(8,128)S(1)} %get-tuple-element.238, bf16[2,896,2,128,1]{3,2,1,0,4:T(2,128)(2,1)} %bitcast.127), kind=kOutput, calls=%fused_computation.21.clone.1 | convolution fusion | flops 947388416 | bytes 16662528 | tf_op jit(solution)/shard_map/while/body/eval_jaxpr/bkgtj,bjkd->btkgd/dot_general | solution.py:120
  252.7 2.0 gather_fusion
  257.3 2.9 squeeze.42
  260.2 2.3 constant_dynamic-slice_fusion.4
  263.7 11.2 %fusion.92 = (f32[2,2,8,128]{3,2,1,0:T(8,128)S(1)}, f32[2,2,8,128,896]{3,4,2,1,0:T(8,128)}) fusion(pred[2,128,896]{1,2,0:T(8,128)(4,1)S(1)} %broadcast_select_fusion.4, bf16[2,128,2,8,128]{1,4,3,2,0:T(8,128)(2,1)} %bitcast.124, bf16[2,896,2,128,1]{3,2,1,0,4:T(2,128)(2,1)} %bitcast.126), kind=kOutput, calls=%fused_computation.123.clone.1 | convolution fusion | flops 954205056 | bytes 16891904 | tf_op jit(solution)/shard_map/while/body/eval_jaxpr/sub | solution.py:118
  276.0 7.0 %fusion.93 = bf16[2,2,128,8,128]{4,2,3,1,0:T(8,128)(2,1)S(1)} fusion(f32[2,2,8,128,896]{3,4,2,1,0:T(8,128)} %get-tuple-element.237, f32[2,2,8,128]{3,2,1,0:T(8,128)S(1)} %get-tuple-element.238, bf16[2,896,2,128,1]{3,2,1,0,4:T(2,128)(2,1)} %bitcast.127), kind=kOutput, calls=%fused_computation.21.clone.1 | convolution fusion | flops 947388416 | bytes 16662528 | tf_op jit(solution)/shard_map/while/body/eval_jaxpr/bkgtj,bjkd->btkgd/dot_general | solution.py:120
  283.2 12.7 %psum.7 = f32[16,128]{1,0:T(8,128)} all-reduce(f32[16,128]{1,0:T(8,128)S(1)} %bitcast.132), channel_id=1, replica_groups=mesh['beam'=8,'mp'=4] {'mp'}, use_global_device_ids=true, to_apply=%region_8.12 | all-reduce | flops 2048 | bytes 16384 | tf_op jit(solution)/shard_map/psum | solution.py:137
  (212 shorter events, 53.8 us)
Async XLA Ops:
  0.6 4.0 %copy-start = (bf16[16,2,128,256]{3,2,1,0:T(8,128)(2,1)S(1)}, bf16[16,2,128,256]{3,2,1,0:T(8,128)(2,1)}, u32[]{:S(2)}) copy-start(bf16[16,2,128,256]{3,2,1,0:T(8,128)(2,1)} %param.19) | copy-start | bytes 6291460
  5.3 5.6 %copy-start.3 = (s32[16,5]{0,1:T(8,128)S(1)}, s32[16,5]{0,1:T(8,128)}, u32[]{:S(2)}) copy-start(s32[16,5]{0,1:T(8,128)} %param.22) | copy-start | bytes 964
  6.4 22.7 %all-to-all-start = ((bf16[8,2,128,256]{3,2,1,0:T(8,128)(2,1)}), bf16[8,2,128,256]{3,2,1,0:T(8,128)(2,1)S(1)}, u32[]{:S(2)}, u32[]{:S(2)}) async-start(bf16[8,2,128,256]{3,2,1,0:T(8,128)(2,1)} %select_select_fusion.1), calls=%async_computation | async-start | bytes 2097152 | tf_op jit(solution)/shard_map/all_to_all | solution.py:57
  11.0 12.3 %copy-start.4 = (s32[16]{0:T(128)S(1)}, s32[16]{0:T(128)}, u32[]{:S(2)}) copy-start(s32[16]{0:T(128)} %param.23) | copy-start | bytes 196
  29.2 1.0 copy-start.1
  30.1 265.8 %all-to-all-start.1 = ((bf16[8,2,128,256]{3,2,1,0:T(8,128)(2,1)}), bf16[8,2,128,256]{3,2,1,0:T(8,128)(2,1)}, u32[]{:S(2)}, u32[]{:S(2)}) async-start(bf16[8,2,128,256]{3,2,1,0:T(8,128)(2,1)} %select_select_fusion), calls=%async_computation.1 | async-start | bytes 2097152 | tf_op jit(solution)/shard_map/all_to_all | solution.py:65
  36.4 1.6 copy-start.2
where the time goes:
time: 302 us; the launch traced here: 299 us
  matrix products  147 us (49%)
  local copies, waits for them, and re-layouts  110 us (36%)
  other arithmetic  19 us (6%)
  blocking collectives  12.7 us (4%)
  starting transfers between devices  8.45 us (3%)
    sub x8, matrix products, attend_pair(): weights = jnp.exp(scores - highest)  89.2 us
    dot_general x8, matrix products, attend_pair(): jnp.einsum('bkgtj,bjkd->btkgd', probabilities, value_row_matrix, preferre...  55.9 us
    squeeze x8, local copies, waits for them, and re-layouts, attend_pair(): block_list[:, :, 0].reshape(pair_size, total_key_count, kv_heads, HEAD_SIZE)  23.3 us
    dynamic_slice x8, local copies, waits for them, and re-layouts, on_device(): lax.map(attend_pair, (fold_pairs(queries), fold_pairs(new_kv), fold_pairs...  18.1 us
    gather x8, local copies, waits for them, and re-layouts, attend_pair(): jnp.take(ancestor_block_store, block_ids, axis=0)  16.4 us
    unnamed x11, local copies, waits for them, and re-layouts  13.3 us
    psum x1, blocking collectives, on_device(): reward = lax.psum(partial_reward, 'mp')  12.7 us
    squeeze x8, local copies, waits for them, and re-layouts, attend_pair(): block_list[:, :, 1].reshape(pair_size, total_key_count, kv_heads, HEAD_SIZE)  9.05 us
  transfers between devices with their start and end apart: 2, of which 0 were waited for; matrix products, arithmetic and copies ran while one was open for 89% of the time, Pallas kernels for 0%

commit v1 on v0

v1 whole, which is shorter than its diff:
```python
import functools
import math

import jax
import jax.numpy as jnp
from jax import lax
from jax.experimental import pallas as pl
from jax.experimental.pallas import tpu as pltpu
from jax.sharding import PartitionSpec as P

HEAD_SIZE = 128
CHILD = 2
LOG2_SCALE = HEAD_SIZE ** (-0.5) * math.log2(math.e)
MASKED = -1e30
LANES_BOTH = 2 * HEAD_SIZE
ANY = pl.BlockSpec(memory_space=pl.ANY)


def find_row(table, start, step, count, own_index, beam_dev):
    def look(i, found):
        beam = table[start + i * step]
        return jnp.where(beam // beam_dev == own_index, beam % beam_dev, found)

    return lax.fori_loop(0, count, look, jnp.int32(0))


def pack_kernel(
    own_ref,
    parent_ref,
    keep_ref,
    weight_ref,
    newest_ref,
    new_ref,
    parent_out,
    keep_out,
    value_buf,
    sum_buf,
    keep_sem,
    key_sem,
    value_sem,
    sum_sem,
    *,
    devices,
    beam_dev,
    keep_dev,
):
    groups = beam_dev // CHILD
    own = own_ref[0]
    tokens = newest_ref.shape[2]
    kv_heads = newest_ref.shape[3] // HEAD_SIZE
    heads = weight_ref.shape[0]
    per_group = heads // kv_heads

    def value_copy(d, row):
        return pltpu.make_async_copy(
            newest_ref.at[row, 1], value_buf.at[d], value_sem.at[d]
        )

    def key_copy(d, row):
        return pltpu.make_async_copy(
            newest_ref.at[row, 0], parent_out.at[d, pl.ds(0, tokens)], key_sem.at[d]
        )

    def keep_copy(d, kept):
        return pltpu.make_async_copy(new_ref.at[kept], keep_out.at[d], keep_sem.at[d])

    @pl.loop(0, devices)
    def _(d):
        row = find_row(parent_ref, d * beam_dev, CHILD, groups, own, beam_dev)
        kept = find_row(keep_ref, d * keep_dev, 1, keep_dev, own, beam_dev)
        value_copy(d, row).start()
        key_copy(d, row).start()
        keep_copy(d, kept).start()

    def sums_copy(d):
        return pltpu.make_async_copy(
            sum_buf.at[d],
            parent_out.at[d, pl.ds(tokens, 2 * per_group)],
            sum_sem.at[d],
        )

    @pl.loop(0, devices)
    def _(d):
        value_copy(d, 0).wait()
        for kv in range(kv_heads):
            total = lax.dot_general(
                weight_ref[kv * per_group : (kv + 1) * per_group],
                value_buf[d, :, kv * HEAD_SIZE : (kv + 1) * HEAD_SIZE],
                (((1,), (1,)), ((), ())),
                preferred_element_type=jnp.float32,
            )
            high = total.astype(jnp.bfloat16)
            low = (total - high.astype(jnp.float32)).astype(jnp.bfloat16)
            lanes = slice(kv * tokens, (kv + 1) * tokens)
            sum_buf[d, :per_group, lanes] = high
            sum_buf[d, per_group:, lanes] = low
        sums_copy(d).start()

    @pl.loop(0, devices)
    def _(d):
        key_copy(d, 0).wait()
        keep_copy(d, 0).wait()
        sums_copy(d).wait()


def online_step(scores, sums, state, pair):
    highest, top, bottom = state
    scores = scores.reshape(-1, 8, scores.shape[-1])
    sums = sums.reshape(scores.shape)
    before = highest[pair]
    after = jnp.maximum(before, jnp.max(scores, axis=0))
    fade = jnp.exp2((before - after) * LOG2_SCALE)
    weights = jnp.exp2((scores - after[None]) * LOG2_SCALE)
    return (
        after,
        top[pair] * fade + jnp.sum(weights * sums, axis=0),
        bottom[pair] * fade + jnp.sum(weights, axis=0),
    )


def query_pair(query_ref, pair):
    start = pair * LANES_BOTH
    return jnp.concatenate(
        [
            query_ref[0, :, start : start + HEAD_SIZE],
            query_ref[0, :, start + HEAD_SIZE : start + LANES_BOTH],
        ],
        axis=0,
    )


def key_scores(keys, query):
    return lax.dot_general(
        keys, query, (((1,), (1,)), ((), ())), preferred_element_type=jnp.float32
    )


def local_kernel(
    block_ids,
    live_count,
    query_ref,
    own_ref,
    store_ref,
    spread_ref,
    state_ref,
    sums_ref,
    *,
    pairs,
    pairs_kv,
):
    beam = pl.program_id(0)
    blocks = store_ref.shape[0]
    tokens = store_ref.shape[2]

    def spread_sums(values, pair):
        return jnp.dot(
            values,
            spread_ref[:, pair * LANES_BOTH : (pair + 1) * LANES_BOTH],
            preferred_element_type=jnp.float32,
        )

    def lanes(pair):
        kv = pair // pairs_kv
        return slice(kv * HEAD_SIZE, (kv + 1) * HEAD_SIZE)

    @pl.when(beam == 0)
    def _():
        @pl.loop(0, blocks)
        def _(block):
            for pair in range(pairs):
                sums_ref[block, pair] = spread_sums(
                    store_ref[block, 1, :, lanes(pair)], pair
                )

    state = (state_ref.at[0, 0], state_ref.at[0, 1], state_ref.at[0, 2])
    state_ref[0, 0] = jnp.full(state_ref.shape[2:], MASKED, jnp.float32)
    state_ref[0, 1] = jnp.zeros(state_ref.shape[2:], jnp.float32)
    state_ref[0, 2] = jnp.zeros(state_ref.shape[2:], jnp.float32)

    def update(pair, scores, sums):
        highest, top, bottom = online_step(scores, sums, state, pair)
        state_ref[0, 0, pair] = highest
        state_ref[0, 1, pair] = top
        state_ref[0, 2, pair] = bottom

    @pl.loop(0, live_count[beam])
    def _(slot):
        block = block_ids[beam, slot]
        for pair in range(pairs):
            scores = key_scores(
                store_ref[block, 0, :, lanes(pair)], query_pair(query_ref, pair)
            )
            update(pair, scores, sums_ref[block, pair])

    shape = (tokens, LANES_BOTH)
    key_pos = lax.broadcasted_iota(jnp.int32, shape, 0)
    token_pos = lax.broadcasted_iota(jnp.int32, shape, 1) % tokens
    allowed = key_pos <= token_pos
    for pair in range(pairs):
        scores = key_scores(own_ref[0, 0, :, lanes(pair)], query_pair(query_ref, pair))
        scores = jnp.where(allowed, scores, MASKED)
        update(pair, scores, spread_sums(own_ref[0, 1, :, lanes(pair)], pair))


def parent_kernel(
    source,
    query_ref,
    state_ref,
    parent_ref,
    select_ref,
    reward_ref,
    sums_ref,
    *,
    pairs,
    pairs_kv,
):
    beam = pl.program_id(0)
    sum_rows = select_ref.shape[0]
    tokens = parent_ref.shape[1] - sum_rows

    @pl.when(beam % CHILD == 0)
    def _():
        for pair in range(pairs):
            kv = pair // pairs_kv
            start = (pair % pairs_kv) * LANES_BOTH
            sums_ref[pair] = lax.dot_general(
                parent_ref[0, pl.ds(tokens, sum_rows), kv * tokens : (kv + 1) * tokens],
                select_ref[:, start : start + LANES_BOTH],
                (((0,), (0,)), ((), ())),
                preferred_element_type=jnp.float32,
            )

    state = (state_ref.at[0, 0], state_ref.at[0, 1], state_ref.at[0, 2])
    total = jnp.zeros((1, tokens), jnp.float32)
    for pair in range(pairs):
        kv = pair // pairs_kv
        scores = key_scores(
            parent_ref[0, pl.ds(0, tokens), kv * HEAD_SIZE : (kv + 1) * HEAD_SIZE],
            query_pair(query_ref, pair),
        )
        highest, top, bottom = online_step(scores, sums_ref[pair], state, pair)
        row_max = jnp.max(highest, axis=0, keepdims=True)
        fade = jnp.exp2((highest - row_max) * LOG2_SCALE)
        ratio = jnp.sum(top * fade, axis=0, keepdims=True) / jnp.sum(
            bottom * fade, axis=0, keepdims=True
        )
        total = total + ratio[:, :tokens] + ratio[:, tokens:]
    reward_ref[pl.ds(beam, 1), :] = total


def place_kernel(source, landed_ref, kept_ref, sems, *, keep_dev):
    def copy(j):
        return pltpu.make_async_copy(
            landed_ref.at[source[j]], kept_ref.at[j], sems.at[j]
        )

    for j in range(keep_dev):
        copy(j).start()
    for j in range(keep_dev):
        copy(j).wait()


def on_device(
    queries,
    new_kv,
    newest_key_value,
    ancestor_block_store,
    parent,
    ancestors,
    ancestor_count,
    keep_list,
    w_reward,
):
    devices = lax.axis_size("beam")
    mp = lax.axis_size("mp")
    own = lax.axis_index("beam")
    beam_dev, _, tokens, kv_width = new_kv.shape
    q_width = queries.shape[2]
    heads = q_width // HEAD_SIZE
    kv_heads = kv_width // HEAD_SIZE
    pairs = heads // 2
    pairs_kv = pairs // kv_heads
    keep_dev = keep_list.shape[0] // devices
    blocks = ancestor_block_store.shape[0]
    slots = ancestors.shape[1]
    per_group = heads // kv_heads
    sum_rows = 2 * per_group

    weight = w_reward.reshape(heads, HEAD_SIZE)
    parent_out, keep_out = pl.pallas_call(
        functools.partial(
            pack_kernel, devices=devices, beam_dev=beam_dev, keep_dev=keep_dev
        ),
        out_shape=(
            jax.ShapeDtypeStruct((devices, tokens + sum_rows, kv_width), jnp.bfloat16),
            jax.ShapeDtypeStruct((devices, 2, tokens, kv_width), jnp.bfloat16),
        ),
        grid_spec=pltpu.PrefetchScalarGridSpec(
            num_scalar_prefetch=3,
            grid=(1,),
            in_specs=[
                pl.BlockSpec((heads, HEAD_SIZE), lambda i, *_: (0, 0)),
                ANY,
                ANY,
            ],
            out_specs=(ANY, ANY),
            scratch_shapes=[
                pltpu.VMEM((devices, tokens, kv_width), jnp.bfloat16),
                pltpu.VMEM((devices, sum_rows, kv_width), jnp.bfloat16),
                pltpu.SemaphoreType.DMA((devices,)),
                pltpu.SemaphoreType.DMA((devices,)),
                pltpu.SemaphoreType.DMA((devices,)),
                pltpu.SemaphoreType.DMA((devices,)),
            ],
        ),
        name="pack",
    )(own.reshape(1), parent, keep_list, weight, newest_key_value, new_kv)

    arrived = lax.all_to_all(parent_out, "beam", split_axis=0, concat_axis=0, tiled=True)
    landed = lax.all_to_all(keep_out, "beam", split_axis=0, concat_axis=0, tiled=True)

    spread = jnp.repeat(weight.T, HEAD_SIZE, axis=1)
    local_ids = ancestors - own * blocks
    state_shape = (beam_dev, 3, pairs, 8, LANES_BOTH)
    state_block = (1,) + state_shape[1:]
    state = pl.pallas_call(
        functools.partial(local_kernel, pairs=pairs, pairs_kv=pairs_kv),
        out_shape=jax.ShapeDtypeStruct(state_shape, jnp.float32),
        grid_spec=pltpu.PrefetchScalarGridSpec(
            num_scalar_prefetch=2,
            grid=(beam_dev,),
            in_specs=[
                pl.BlockSpec((1, tokens, q_width), lambda b, *_: (b, 0, 0)),
                pl.BlockSpec((1, 2, tokens, kv_width), lambda b, *_: (b, 0, 0, 0)),
                pl.BlockSpec(
                    ancestor_block_store.shape,
                    lambda b, *_: (0, 0, 0, 0),
                    pipeline_mode=pl.Buffered(1),
                ),
                pl.BlockSpec(
                    spread.shape, lambda b, *_: (0, 0), pipeline_mode=pl.Buffered(1)
                ),
            ],
            out_specs=pl.BlockSpec(state_block, lambda b, *_: (b, 0, 0, 0, 0)),
            scratch_shapes=[
                pltpu.VMEM((blocks, pairs, tokens, LANES_BOTH), jnp.float32)
            ],
        ),
        name="local",
    )(local_ids, ancestor_count, queries, new_kv, ancestor_block_store, spread)

    own_parents = lax.dynamic_slice(parent, (own * beam_dev,), (beam_dev,))
    source = own_parents // beam_dev
    head_ids = jnp.arange(sum_rows) % per_group
    lane_heads = jnp.arange(per_group * HEAD_SIZE) // HEAD_SIZE
    select = (head_ids[:, None] == lane_heads[None, :]).astype(jnp.bfloat16)
    partial_reward = pl.pallas_call(
        functools.partial(parent_kernel, pairs=pairs, pairs_kv=pairs_kv),
        out_shape=jax.ShapeDtypeStruct((beam_dev, tokens), jnp.float32),
        grid_spec=pltpu.PrefetchScalarGridSpec(
            num_scalar_prefetch=1,
            grid=(beam_dev,),
            in_specs=[
                pl.BlockSpec((1, tokens, q_width), lambda b, *_: (b, 0, 0)),
                pl.BlockSpec(state_block, lambda b, *_: (b, 0, 0, 0, 0)),
                pl.BlockSpec(
                    (1, tokens + sum_rows, kv_width),
                    lambda b, source: (source[b], 0, 0),
                ),
                pl.BlockSpec(
                    select.shape, lambda b, *_: (0, 0), pipeline_mode=pl.Buffered(1)
                ),
            ],
            out_specs=pl.BlockSpec((beam_dev, tokens), lambda b, *_: (0, 0)),
            scratch_shapes=[pltpu.VMEM((pairs, tokens, LANES_BOTH), jnp.float32)],
        ),
        name="parents",
    )(source, queries, state, arrived, select)

    keep_source = (
        lax.dynamic_slice(keep_list, (own * keep_dev,), (keep_dev,)) // beam_dev
    )
    kept_blocks = pl.pallas_call(
        functools.partial(place_kernel, keep_dev=keep_dev),
        out_shape=jax.ShapeDtypeStruct((keep_dev,) + new_kv.shape[1:], new_kv.dtype),
        grid_spec=pltpu.PrefetchScalarGridSpec(
            num_scalar_prefetch=1,
            grid=(1,),
            in_specs=[ANY],
            out_specs=ANY,
            scratch_shapes=[pltpu.SemaphoreType.DMA((keep_dev,))],
        ),
        name="place",
    )(keep_source, landed)

    reward = partial_reward
    for shift in range(1, mp):
        ring = [(i, (i + shift) % mp) for i in range(mp)]
        reward = reward + lax.ppermute(partial_reward, "mp", ring)
    return (reward, kept_blocks)


def solution(mesh):
    placed = (
        P("beam", None, "mp"),
        P("beam", None, None, "mp"),
        P("beam", None, None, "mp"),
        P("beam", None, None, "mp"),
        P(),
        P("beam", None),
        P("beam"),
        P(),
        P("mp"),
    )
    return jax.shard_map(
        on_device,
        mesh=mesh,
        in_specs=placed,
        out_specs=(P("beam", None), P("beam", None, None, "mp")),
        check_vma=False,
    )
```

time: 302 us -> 177 us (0.59)
  matrix products: 147 us -> 0 us
  Pallas kernels: 0 us -> 144 us
  local copies, waits for them, and re-layouts: 110 us -> 2.47 us
  other arithmetic: 19 us -> 3.76 us
  blocking collectives: 12.7 us -> 0 us
  waiting for transfers between devices: 0.01 us -> 10.8 us
  starting transfers between devices: 8.45 us -> 14.7 us
    pallas_call x0 -> x4, Pallas kernels: none -> 144 us  [the longest x1 50.5 us: on_device(): pl.pallas_call(functools.partial(pack_kernel, devices=devices, beam_dev=b...]
    sub x8 -> x0, matrix products: 89.2 us -> none  [attend_pair(): weights = jnp.exp(scores - highest)]
    dot_general x16 -> x0, matrix products: 57.9 us -> none  [the longest x8 55.9 us: attend_pair(): jnp.einsum('bkgtj,bjkd->btkgd', probabilities, value_row_matrix, preferre...]
    squeeze x17 -> x0, local copies, waits for them, and re-layouts: 32.3 us -> none  [the longest x8 23.3 us: attend_pair(): block_list[:, :, 0].reshape(pair_size, total_key_count, kv_heads, HEAD_SIZE)]
    gather x14 -> x0, local copies, waits for them, and re-layouts: 25.1 us -> none  [the longest x8 16.4 us: attend_pair(): jnp.take(ancestor_block_store, block_ids, axis=0)]
    dynamic_slice x8 -> x0, local copies, waits for them, and re-layouts: 18.1 us -> none  [on_device(): lax.map(attend_pair, (fold_pairs(queries), fold_pairs(new_kv), fold_pairs...]
    select_n x54 -> x4, other arithmetic: 15.4 us -> 1.18 us  [the longest x1 0.6 us: on_device(): source = own_parents // beam_dev]
    psum x1 -> x0, blocking collectives: 12.7 us -> none  [on_device(): reward = lax.psum(partial_reward, 'mp')]
  transfers between devices with their start and end apart: 2 -> 5, of which waited for: 0 -> 3; matrix products, arithmetic and copies ran while one was open for 89% -> 3% of each run, Pallas kernels for 0% -> 34%
where the time goes in v1:
time: 177 us; the launch traced here: 176 us
  Pallas kernels  144 us (81%)
  starting transfers between devices  14.7 us (8%)
  waiting for transfers between devices  10.8 us (6%)
  other arithmetic  3.76 us (2%)
  local copies, waits for them, and re-layouts  2.47 us (1%)
    pallas_call x1, Pallas kernels, on_device(): pl.pallas_call(functools.partial(pack_kernel, devices=devices, beam_dev=b...  50.5 us
    pallas_call x1, Pallas kernels, on_device(): pl.pallas_call(functools.partial(local_kernel, pairs=pairs, pairs_kv=pair...  41.5 us
    pallas_call x1, Pallas kernels, on_device(): pl.pallas_call(functools.partial(place_kernel, keep_dev=keep_dev), out_sh...  33.6 us
    pallas_call x1, Pallas kernels, on_device(): pl.pallas_call(functools.partial(parent_kernel, pairs=pairs, pairs_kv=pai...  18.1 us
    all_to_all x1, waiting for transfers between devices, on_device(): lax.all_to_all(parent_out, 'beam', split_axis=0, concat_axis=0, tiled=True)  8.87 us
    ppermute x3, starting transfers between devices, on_device(): reward = reward + lax.ppermute(partial_reward, 'mp', ring)  5.52 us
    all_to_all x1, starting transfers between devices, on_device(): lax.all_to_all(keep_out, 'beam', split_axis=0, concat_axis=0, tiled=True)  4.93 us
    all_to_all x1, starting transfers between devices, on_device(): lax.all_to_all(parent_out, 'beam', split_axis=0, concat_axis=0, tiled=True)  4.27 us
  transfers between devices with their start and end apart: 5, of which 3 were waited for; matrix products, arithmetic and copies ran while one was open for 3% of the time, Pallas kernels for 34%

profile of v1, /device:TPU:2, one launch (start us, length us, event | category | flops | bytes accessed | tf_op | source)
XLA Modules:
  0.0 176.1 jit_solution(3470635358119230200)
XLA Ops:
  0.6 0.0 copy-start.3
  0.6 50.5 %pack.1 = (bf16[8,144,256]{2,1,0:T(8,128)(2,1)}, bf16[8,2,128,256]{3,2,1,0:T(8,128)(2,1)}) custom-call(s32[1]{0:T(128)} %bitcast.2.own_ref, s32[128]{0:T(128)} %parent_ref.1, s32[64]{0:T(128)} %keep_ref.1, bf16[16,128]{1,0:T(8,128)(2,1)} %bitcast.10, bf16[16,2,128,256]{3,2,1,0:T(8,128)(2,1)} %newest_ref.1, bf16[16,2,128,256]{3,2,1,0:T(8,128)(2,1)} %new_ref.1), custom_call_target="tpu_custom_call" | custom-call | tf_op jit(solution)/shard_map/pack/pallas_call | solution.py:290
  51.2 0.0 copy-start.2
  51.2 4.3 %all-to-all-start = ((bf16[8,144,256]{2,1,0:T(8,128)(2,1)}), bf16[8,144,256]{2,1,0:T(8,128)(2,1)S(1)}, u32[]{:S(2)}, u32[]{:S(2)}) async-start(bf16[8,144,256]{2,1,0:T(8,128)(2,1)} %get-tuple-element.4), calls=%async_computation | async-start | bytes 1179648 | tf_op jit(solution)/shard_map/all_to_all | solution.py:319
  55.5 0.0 copy-done.3
  55.5 0.1 copy.13
  55.5 8.9 %all-to-all-done.parent_ref = bf16[8,144,256]{2,1,0:T(8,128)(2,1)S(1)} async-done(((bf16[8,144,256]{2,1,0:T(8,128)(2,1)}), bf16[8,144,256]{2,1,0:T(8,128)(2,1)S(1)}, u32[]{:S(2)}, u32[]{:S(2)}) %all-to-all-start) | async-done | bytes 589856 | tf_op jit(solution)/shard_map/all_to_all | solution.py:319
  64.4 0.0 copy-start.1
  64.4 4.9 %all-to-all-start.1 = ((bf16[8,2,128,256]{3,2,1,0:T(8,128)(2,1)}), bf16[8,2,128,256]{3,2,1,0:T(8,128)(2,1)S(1)}, u32[]{:S(2)}, u32[]{:S(2)}) async-start(bf16[8,2,128,256]{3,2,1,0:T(8,128)(2,1)} %get-tuple-element.5), calls=%async_computation.1 | async-start | bytes 2097152 | tf_op jit(solution)/shard_map/all_to_all | solution.py:320
  69.3 0.6 broadcast_subtract_fusion.block_ids
  69.9 0.0 copy-done.2
  69.9 0.1 copy.15
  70.1 0.3 broadcast_in_dim.2
  70.4 0.9 copy.18
  71.4 0.0 copy-start.4
  71.4 41.5 %local.1.state_ref = f32[16,3,8,8,256]{4,3,2,1,0:T(8,128)} custom-call(s32[16,5]{1,0:T(8,128)} %broadcast_subtract_fusion.block_ids, s32[16]{0:T(128)} %live_count.1, bf16[16,128,2048]{2,1,0:T(8,128)(2,1)} %query_ref.3, bf16[16,2,128,256]{3,2,1,0:T(8,128)(2,1)} %new_ref.1, bf16[12,2,128,256]{3,2,1,0:T(8,128)(2,1)} %store_ref.1, bf16[128,2048]{1,0:T(8,128)(2,1)} %bitcast.8), custom_call_target="tpu_custom_call" | custom-call | tf_op jit(solution)/shard_map/local/pallas_call | solution.py:326
  112.9 0.0 copy-done.1
  112.9 0.0 copy-done.4
  112.9 0.6 and_select_fusion.2.source
  113.5 0.7 compare_convert_fusion.select_ref
  114.2 0.0 copy-start.5
  114.2 18.1 %parents.1 = f32[16,128]{1,0:T(8,128)} custom-call(s32[16]{0:T(128)} %and_select_fusion.2.source, bf16[16,128,2048]{2,1,0:T(8,128)(2,1)} %query_ref.3, f32[16,3,8,8,256]{4,3,2,1,0:T(8,128)} %local.1.state_ref, bf16[8,144,256]{2,1,0:T(8,128)(2,1)} %copy-done.1, bf16[16,1024]{1,0:T(8,128)(2,1)} %compare_convert_fusion.select_ref), custom_call_target="tpu_custom_call" | custom-call | tf_op jit(solution)/shard_map/parents/pallas_call | solution.py:357
  132.3 1.6 collective-permute-start
  133.8 2.6 %collective-permute-start.1 = (f32[16,128]{1,0:T(8,128)}, f32[16,128]{1,0:T(8,128)S(1)}, u32[]{:S(2)}, u32[]{:S(2)}) collective-permute-start(f32[16,128]{1,0:T(8,128)} %parents.1), channel_id=1, source_target_pairs={{0,2},{1,3},{2,0},{3,1},{4,6},{5,7},{6,4},{7,5},{8,10},{9,11},{10,... | collective-permute-start | bytes 24584 | tf_op jit(solution)/shard_map/ppermute | solution.py:399
  136.4 1.4 collective-permute-start.2
  137.8 0.0 copy-done.5
  137.8 0.6 and_select_fusion.source
  138.4 0.0 collective-permute-done
  138.4 0.2 collective-permute-done.1
  138.6 1.7 collective-permute-done.2
  140.3 1.3 add_add_fusion
  141.6 0.0 all-to-all-done.1.landed_ref
  141.6 0.0 copy-start
  141.6 1.0 copy-done
  142.5 33.6 %place.1 = bf16[8,2,128,256]{3,2,1,0:T(8,128)(2,1)} custom-call(s32[8]{0:T(128)} %and_select_fusion.source, bf16[8,2,128,256]{3,2,1,0:T(8,128)(2,1)} %copy-done), custom_call_target="tpu_custom_call" | custom-call | tf_op jit(solution)/shard_map/place/pallas_call | solution.py:383
  (2 shorter events, 0.0 us)
Async XLA Ops:
  0.6 54.8 %copy-start.3 = (s32[16,5]{0,1:T(8,128)S(1)}, s32[16,5]{0,1:T(8,128)}, u32[]{:S(2)}) copy-start(s32[16,5]{0,1:T(8,128)} %param.14) | copy-start | bytes 964
  51.2 18.8 %copy-start.2 = (bf16[2048]{0:T(1024)(128)(2,1)S(1)}, bf16[2048]{0:T(1024)(128)(2,1)}, u32[]{:S(2)}) copy-start(bf16[2048]{0:T(1024)(128)(2,1)} %param.17) | copy-start | bytes 12292
  51.2 13.2 %all-to-all-start = ((bf16[8,144,256]{2,1,0:T(8,128)(2,1)}), bf16[8,144,256]{2,1,0:T(8,128)(2,1)S(1)}, u32[]{:S(2)}, u32[]{:S(2)}) async-start(bf16[8,144,256]{2,1,0:T(8,128)(2,1)} %get-tuple-element.4), calls=%async_computation | async-start | bytes 1179648 | tf_op jit(solution)/shard_map/all_to_all | solution.py:319
  64.4 48.5 %copy-start.1 = (bf16[8,144,256]{2,1,0:T(8,128)(2,1)}, bf16[8,144,256]{2,1,0:T(8,128)(2,1)S(1)}, u32[]{:S(2)}) copy-start(bf16[8,144,256]{2,1,0:T(8,128)(2,1)S(1)} %all-to-all-done.parent_ref) | copy-start | bytes 1769476
  64.4 77.2 %all-to-all-start.1 = ((bf16[8,2,128,256]{3,2,1,0:T(8,128)(2,1)}), bf16[8,2,128,256]{3,2,1,0:T(8,128)(2,1)S(1)}, u32[]{:S(2)}, u32[]{:S(2)}) async-start(bf16[8,2,128,256]{3,2,1,0:T(8,128)(2,1)} %get-tuple-element.5), calls=%async_computation.1 | async-start | bytes 2097152 | tf_op jit(solution)/shard_map/all_to_all | solution.py:320
  71.4 41.5 %copy-start.4 = (s32[128]{0:T(128)S(1)}, s32[128]{0:T(128)}, u32[]{:S(2)}) copy-start(s32[128]{0:T(128)} %parent_ref.1) | copy-start | bytes 1540
  114.2 23.6 %copy-start.5 = (s32[64]{0:T(128)S(1)}, s32[64]{0:T(128)}, u32[]{:S(2)}) copy-start(s32[64]{0:T(128)} %keep_ref.1) | copy-start | bytes 772
  132.3 6.1 %collective-permute-start = (f32[16,128]{1,0:T(8,128)}, f32[16,128]{1,0:T(8,128)S(1)}, u32[]{:S(2)}, u32[]{:S(2)}) collective-permute-start(f32[16,128]{1,0:T(8,128)} %parents.1), channel_id=1, source_target_pairs={{0,1},{1,2},{2,3},{3,0},{4,5},{5,6},{6,7},{7,4},{8,9},{9,10},{10,1... | collective-permute-start | bytes 24584 | tf_op jit(solution)/shard_map/ppermute | solution.py:399
  133.8 4.8 %collective-permute-start.1 = (f32[16,128]{1,0:T(8,128)}, f32[16,128]{1,0:T(8,128)S(1)}, u32[]{:S(2)}, u32[]{:S(2)}) collective-permute-start(f32[16,128]{1,0:T(8,128)} %parents.1), channel_id=1, source_target_pairs={{0,2},{1,3},{2,0},{3,1},{4,6},{5,7},{6,4},{7,5},{8,10},{9,11},{10,... | collective-permute-start | bytes 24584 | tf_op jit(solution)/shard_map/ppermute | solution.py:399
  136.4 3.9 %collective-permute-start.2 = (f32[16,128]{1,0:T(8,128)}, f32[16,128]{1,0:T(8,128)S(1)}, u32[]{:S(2)}, u32[]{:S(2)}) collective-permute-start(f32[16,128]{1,0:T(8,128)} %parents.1), channel_id=1, source_target_pairs={{0,3},{1,0},{2,1},{3,2},{4,7},{5,4},{6,5},{7,6},{8,11},{9,8},{10,9... | collective-permute-start | bytes 24584 | tf_op jit(solution)/shard_map/ppermute | solution.py:399
  141.6 1.0 copy-start
